TPU v7x, 256 devices: a whole 4x4x8 slice. The times are simulated.
256 devices in a mesh: seq: 64 (over y, z, core), tensor: 4 (over x).
Axes of the slice: x: 4, y: 4, z: 8, core: 2. Of those that a mesh axis runs over, the one named last changes fastest.
Arguments:
- tokens: bfloat16 [32768, 3840], P('seq', 'tensor'), may hold values from -6 to 6
- w_query: bfloat16 [3840, 2048], P(None, 'tensor'), may hold values from -0.09375 to 0.09375
- w_key: bfloat16 [3840, 1024], P(None, 'tensor'), may hold values from -0.09375 to 0.09375
- w_value: bfloat16 [3840, 1024], P(None, 'tensor'), may hold values from -0.09375 to 0.09375
- query_gain: float32 [256], replicated, may hold values from 0.1 to 1.9
- key_gain: float32 [256], replicated, may hold values from 0.1 to 1.9
- adapter_down: bfloat16 [64, 64, 3840], P('seq', None, 'tensor'), may hold values from -0.09375 to 0.09375
- adapter_up: bfloat16 [64, 64, 2048], P('seq', None, 'tensor'), may hold values from -0.75 to 0.75
- adapter_ids: int32 [32768, 1], P('seq'), may hold values from 0 to 63; in each aligned block of 512 rows (0 to 511, 512 to 1023, ...) at most 16 rows name the same one
- doc_ids: int32 [32768], P('seq'), may hold values from 0 to 63, never falling along the last dimension, each value on 1 to 4096 neighbouring positions
- cotangent: bfloat16 [32768, 2048], P('seq', 'tensor'), may hold values from -6 to 6
Outputs:
- attended: bfloat16 [32768, 2048], P('seq', 'tensor')
- grad_up: float32 [64, 64, 2048], P('seq', None, 'tensor')
Inputs may be any that keep to these rules, and one draw needn't show every extreme that they name: `adapter_ids`: within the 512 tokens of one device no adapter is named by more than 16 tokens; in every draw some adapter is named by exactly 16 tokens of some device. `doc_ids`: document numbers never fall along the slab; each document has 1 to 4096 tokens and one has exactly 4096.
All inputs are finite; a program needn't handle non-finite values.
Results may differ from a plain program's by a relative error of at most 0.0088.
Values may be sent and summed in bfloat16 or wider, within the bound.
A program may use at most 128 MiB of HBM per device.

v0:
```python
import math
import jax
import jax.numpy as jnp
from jax import lax
from jax.sharding import PartitionSpec as P

HD = 256
R = 64
WINDOW = 1024
ADAPTERS = 64
CAP = 16


def passed_along(value, axis, steps):
    count = lax.axis_size(axis)
    first, last = (max(0, -steps), min(count, count - steps))
    return lax.ppermute(value, axis, [(source, source + steps) for source in range(first, last)])


def normalize(pre_field, gain_vec):
    mean_sq = jnp.mean(pre_field * pre_field, axis=-1, keepdims=True)
    return pre_field * lax.rsqrt(mean_sq + 1e-06) * gain_vec


def rotate(pre_field, positions):
    half_dim = pre_field.shape[-1] // 2
    frequency = jnp.exp(
        jnp.arange(half_dim, dtype=jnp.float32) * (-2.0 * math.log(10000.0) / pre_field.shape[-1])
    )
    angles = positions.astype(jnp.float32)[:, None] * frequency[None, :]
    cosine = jnp.cos(angles)[:, None, :]
    sine_part = jnp.sin(angles)[:, None, :]
    lower_half = pre_field[..., :half_dim]
    second = pre_field[..., half_dim:]
    return jnp.concatenate(
        [lower_half * cosine - second * sine_part, second * cosine + lower_half * sine_part],
        axis=-1,
    )


def shape_query(pre_field, gain_vec, positions):
    return rotate(normalize(pre_field, gain_vec), positions)


def attend(queries, key_rows, values, upstream, allowed):
    score_scale = 1.0 / math.sqrt(queries.shape[-1])
    scores = (
        jnp.einsum("tngd,knd->ngtk", queries, key_rows, preferred_element_type=jnp.float32)
        * score_scale
    )
    weights = jnp.where(allowed[None, None], jnp.exp(scores), 0.0)
    probs = weights / jnp.sum(weights, axis=-1, keepdims=True)
    probs_low = probs.astype(jnp.bfloat16)
    attended = jnp.einsum("ngtk,knd->tngd", probs_low, values, preferred_element_type=jnp.float32)
    dprobs = jnp.einsum("tngd,knd->ngtk", upstream, values, preferred_element_type=jnp.float32)
    delta = jnp.sum(probs * dprobs, axis=-1, keepdims=True)
    dscores = (probs * (dprobs - delta) * score_scale).astype(jnp.bfloat16)
    dqueries = jnp.einsum("ngtk,knd->tngd", dscores, key_rows, preferred_element_type=jnp.float32)
    return (attended.astype(jnp.bfloat16), dqueries)


def local(
    tokens,
    w_query,
    w_key,
    w_value,
    query_gain,
    key_gain,
    adapter_down,
    adapter_up,
    adapter_ids,
    doc_ids,
    cotangent,
):
    tok_count = tokens.shape[0]
    feat_width = tokens.shape[1]
    q_width = w_query.shape[1]
    kv_width = w_key.shape[1]
    local_heads = q_width // HD
    kv_heads = kv_width // HD
    head_group = local_heads // kv_heads
    positions = lax.axis_index("seq") * tok_count + jnp.arange(tok_count, dtype=jnp.int32)
    shard_cols = lax.all_gather(tokens, "tensor", axis=1, tiled=True)
    query_lin = jnp.dot(shard_cols, w_query, preferred_element_type=jnp.float32)
    key_lin = jnp.dot(shard_cols, w_key, preferred_element_type=jnp.float32)
    value_lin = jnp.dot(shard_cols, w_value, preferred_element_type=jnp.float32)
    token_adapter = adapter_ids[:, 0]
    chosen = token_adapter[:, None] == jnp.arange(ADAPTERS, dtype=jnp.int32)[None, :]
    before = jnp.cumsum(chosen.astype(jnp.int32), axis=0) - 1
    slot_rank = jnp.sum(jnp.where(chosen, before, 0), axis=1)
    slot_index = token_adapter * CAP + slot_rank
    dispatch = (slot_index[None, :] == jnp.arange(ADAPTERS * CAP, dtype=jnp.int32)[:, None]).astype(
        jnp.bfloat16
    )
    outgoing = jnp.dot(dispatch, tokens, preferred_element_type=jnp.float32).astype(jnp.bfloat16)
    all_down, all_up = (
        lax.all_gather(adapter_down, "seq", axis=0, tiled=True),
        lax.all_gather(adapter_up, "seq", axis=0, tiled=True),
    )
    slot_rows = outgoing.reshape(ADAPTERS, CAP, feat_width)
    partial_low = jnp.einsum(
        "acd,ard->acr", slot_rows, all_down, preferred_element_type=jnp.float32
    )
    slot_low = lax.psum(partial_low, "tensor").astype(jnp.bfloat16)
    slot_lift = jnp.einsum(
        "acr,are->ace", slot_low, all_up, preferred_element_type=jnp.float32
    ).astype(jnp.bfloat16)
    lifted = jnp.einsum(
        "st,se->te",
        dispatch,
        slot_lift.reshape(ADAPTERS * CAP, q_width),
        preferred_element_type=jnp.float32,
    ).astype(jnp.bfloat16)
    lowrank = jnp.einsum(
        "st,sr->tr",
        dispatch,
        slot_low.reshape(ADAPTERS * CAP, R),
        preferred_element_type=jnp.float32,
    ).astype(jnp.bfloat16)
    query_pre = (query_lin + lifted.astype(jnp.float32)).reshape(tok_count, local_heads, HD)
    queries, query_back = jax.vjp(
        lambda pre_query: shape_query(pre_query, query_gain, positions), query_pre
    )
    queries = queries.astype(jnp.bfloat16).reshape(tok_count, kv_heads, head_group, HD)
    key_rows = shape_query(key_lin.reshape(tok_count, kv_heads, HD), key_gain, positions).astype(
        jnp.bfloat16
    )
    values = value_lin.astype(jnp.bfloat16).reshape(tok_count, kv_heads, HD)
    rim_count = WINDOW // tok_count
    key_list = []
    value_list = []
    doc_list = []
    place_list = []
    for distance in range(rim_count, 0, -1):
        far_keys, far_values, far_docs = passed_along((key_rows, values, doc_ids), "seq", distance)
        key_list.append(far_keys)
        value_list.append(far_values)
        doc_list.append(far_docs)
        place_list.append(positions - distance * tok_count)
    key_list.append(key_rows)
    value_list.append(values)
    doc_list.append(doc_ids)
    place_list.append(positions)
    window_keys = jnp.concatenate(key_list, axis=0)
    window_values = jnp.concatenate(value_list, axis=0)
    key_docs = jnp.concatenate(doc_list, axis=0)
    key_pos = jnp.concatenate(place_list, axis=0)
    key_gap = positions[:, None] - key_pos[None, :]
    allowed = (
        (doc_ids[:, None] == key_docs[None, :])
        & (key_gap >= 0)
        & (key_gap < WINDOW)
        & (key_pos[None, :] >= 0)
    )
    upstream = cotangent.reshape(tok_count, kv_heads, head_group, HD)
    block_out, dqueries = attend(queries, window_keys, window_values, upstream, allowed)
    attended = block_out.reshape(tok_count, q_width)
    (dquery_pre,) = query_back(dqueries.reshape(tok_count, local_heads, HD))
    dquery_pre = dquery_pre.reshape(tok_count, q_width).astype(jnp.bfloat16)
    out_low = jnp.dot(dispatch, lowrank, preferred_element_type=jnp.float32).astype(jnp.bfloat16)
    out_grad = jnp.dot(dispatch, dquery_pre, preferred_element_type=jnp.float32).astype(
        jnp.bfloat16
    )
    slot_low_rows = out_low.reshape(ADAPTERS, CAP, R)
    slot_grad_rows = out_grad.reshape(ADAPTERS, CAP, q_width)
    grad_up = lax.psum_scatter(
        jnp.einsum(
            "acr,ace->are", slot_low_rows, slot_grad_rows, preferred_element_type=jnp.float32
        ),
        "seq",
        scatter_dimension=0,
        tiled=True,
    )
    return (attended, grad_up)


def solution(mesh):
    in_specs = (
        P("seq", "tensor"),
        P(None, "tensor"),
        P(None, "tensor"),
        P(None, "tensor"),
        P(),
        P(),
        P("seq", None, "tensor"),
        P("seq", None, "tensor"),
        P("seq", None),
        P("seq"),
        P("seq", "tensor"),
    )
    out_specs = (P("seq", "tensor"), P("seq", None, "tensor"))
    return jax.shard_map(local, mesh=mesh, in_specs=in_specs, out_specs=out_specs, check_vma=False)
```

profile of v0, /device:TPU:2, one launch (start us, length us, event | category | flops | bytes accessed | tf_op | source)
XLA Modules:
  0.0 409.1 jit_solution(11032409171625994337)
XLA Ops:
  9.4 1.7 collective-permute-start.3
  11.2 4.0 collective-permute-start.2
  15.9 1.2 reduce-window.6
  17.4 0.8 fusion.59
  18.9 1.0 multiply_cosine_fusion
  19.9 3.7 fusion.24
  23.7 4.0 copy.40
  27.7 2.5 fusion.16
  30.2 30.4 %all-gather.4.cloned.1.call-done = bf16[512,3840]{0,1:T(8,128)(2,1)} async-done(((bf16[512,960]{0,1:T(8,128)(2,1)}), bf16[512,3840]{0,1:T(8,128)(2,1)}) %all-gather.4.cloned.1.call-update) | async-done | bytes 3932176 | tf_op jit(solution)/shard_map/all_gather | solution.py:83
  60.7 3.5 multiply_reduce_fusion.2
  64.3 1.2 fusion.55
  66.2 2.3 collective-permute-start.5
  68.5 3.8 collective-permute-start.4
  72.3 1.9 fusion.34
  74.2 4.0 collective-permute-start.1
  78.2 2.8 collective-permute-start
  81.0 66.8 %all-gather.6.cloned.1.call-done = bf16[64,64,960]{2,1,0:T(8,128)(2,1)} async-done(((bf16[1,64,960]{2,1,0:T(8,128)(2,1)}), bf16[64,64,960]{2,1,0:T(8,128)(2,1)}) %all-gather.6.cloned.1.call-update) | async-done | bytes 7864336 | tf_op jit(solution)/shard_map/all_gather | solution.py:97
  147.8 6.3 %fusion.73 = f32[64,16,64]{2,1,0:T(8,128)S(1)} fusion(bf16[64,16,960]{2,1,0:T(8,128)(2,1)} %bitcast.128, bf16[64,64,960]{2,1,0:T(8,128)(2,1)} %all-gather.6.cloned.1.call-done), kind=kOutput, calls=%fused_computation.106 | convolution fusion | flops 125829120 | bytes 10092544 | tf_op jit(solution)/shard_map/acd,ard->acr/dot_general | solution.py:101
  154.1 20.2 %all-reduce.3 = bf16[64,16,64]{2,1,0:T(8,128)(2,1)S(1)} all-reduce(f32[64,16,64]{2,1,0:T(8,128)S(1)} %fusion.73), channel_id=1, replica_groups=mesh['seq'=64,'tensor'=4] {'tensor'}, use_global_device_ids=true, to_apply=%region_4.5 | all-reduce | flops 65536 | bytes 393216 | tf_op jit(solution)/shard_map/psum | solution.py:104
  174.4 52.3 %all-gather.8.cloned.1.call-done = bf16[64,64,512]{2,1,0:T(8,128)(2,1)} async-done(((bf16[1,64,512]{2,1,0:T(8,128)(2,1)}), bf16[64,64,512]{2,1,0:T(8,128)(2,1)}) %all-gather.8.cloned.1.call-update) | async-done | bytes 4194320 | tf_op jit(solution)/shard_map/all_gather | solution.py:98
  226.7 3.0 convolution_convert_fusion
  229.7 0.8 fusion.30
  230.5 0.8 copy-done.8
  231.2 2.3 multiply_reduce_fusion.1
  233.9 0.9 fusion.35
  235.3 3.1 fusion.5
  238.5 4.4 %fusion = (f32[2,512]{1,0:T(2,128)S(1)}, f32[1536,512,2]{1,0,2:T(8,128)S(1)}) fusion(f32[2,512]{1,0:T(2,128)S(1)} %get-tuple-element.20, f32[1536,512,2]{1,0,2:T(8,128)S(1)} %get-tuple-element.21, pred[512,1536]{0,1:T(8,128)(4,1)S(1)} %copy-done.2, bf16[64,2,8,256]{3,2,1,0:T(8,128)(2,1)S(1)} %bitcast.139, bf16[512,1,256]{2,0,1:T(8,128)(2,1)} %fusion.34, ...), kind=kOutput, calls=%fused_computation.3 | convolution fusion | flops 815528960 | bytes 14688256 | tf_op jit(solution)/shard_map/tngd,knd->ngtk/dot_general | solution.py:55
  242.9 3.8 fusion.26
  248.4 4.5 %fusion.74 = f32[64,64,512]{2,1,0:T(8,128)} fusion(bf16[64,16,64]{2,1,0:T(8,128)(2,1)S(1)} %bitcast.130, bf16[64,16,512]{2,1,0:T(8,128)(2,1)S(1)} %bitcast.129), kind=kOutput, calls=%fused_computation.107 | convolution fusion | flops 67108864 | bytes 9568256 | tf_op jit(solution)/shard_map/acr,ace->are/dot_general | solution.py:167
  253.0 5.2 %fusion.31 = bf16[256,2,512]{2,0,1:T(8,128)(2,1)S(1)} fusion(f32[2,512]{1,0:T(2,128)S(1)} %get-tuple-element.20, f32[1536,512,2]{1,0,2:T(8,128)} %copy-done.11, pred[512,1536]{0,1:T(8,128)(4,1)S(1)} %copy-done.2, bf16[512,1,256]{2,0,1:T(8,128)(2,1)} %fusion.34, bf16[512,1,256]{2,0,1:T(8,128)(2,1)} %collective-permute-done.1, ...), kind=kOutput, calls=%fused_computation.35 | convolution fusion | flops 814219264 | bytes 8392704 | tf_op jit(solution)/shard_map/ngtk,knd->tngd/dot_general | solution.py:54
  258.2 1.0 copy.52
  259.2 143.4 %reduce-scatter.2.cloned.1.call-done = f32[1,64,512]{2,1,0:T(8,128)} async-done(((f32[64,64,512]{2,1,0:T(8,128)}), f32[1,64,512]{2,1,0:T(8,128)}) %reduce-scatter.2.cloned.1.call-update) | async-done | bytes 131088 | tf_op jit(solution)/shard_map/reduce_scatter | solution.py:166
  (63 shorter events, 7.4 us)
Async XLA Ops:
  7.2 53.5 %copy-start = (bf16[3840,256]{1,0:T(8,128)(2,1)S(1)}, bf16[3840,256]{1,0:T(8,128)(2,1)}, u32[]{:S(2)}) copy-start(bf16[3840,256]{1,0:T(8,128)(2,1)} %param.13) | copy-start | bytes 5898244
  7.2 53.5 %all-gather.4.cloned.1.call-start = ((), (), s32[]{:S(2)}) async-start(), calls=%async_computation.1 | async-start | bytes 4915200 | tf_op jit(solution)/shard_map/all_gather | solution.py:83
  7.9 139.9 %all-gather.6.cloned.1.call-start = ((), (), s32[]{:S(2)}) async-start(), calls=%async_computation.2 | async-start | bytes 8519680 | tf_op jit(solution)/shard_map/all_gather | solution.py:97
  8.7 218.0 %all-gather.8.cloned.1.call-start = ((), (), s32[]{:S(2)}) async-start(), calls=%async_computation.3 | async-start | bytes 4259840 | tf_op jit(solution)/shard_map/all_gather | solution.py:98
  9.4 393.2 %reduce-scatter.2.cloned.1.call-start = ((), (), s32[]{:S(2)}) async-start(), calls=%async_computation.4 | async-start | bytes 8519680 | tf_op jit(solution)/shard_map/reduce_scatter | solution.py:166
  9.4 18.2 %collective-permute-start.3 = (s32[512]{0:T(512)}, s32[512]{0:T(512)S(1)}, u32[]{:S(2)}, u32[]{:S(2)}) collective-permute-start(s32[512]{0:T(512)} %param.20), channel_id=1, source_target_pairs={{0,4},{4,8},{8,12},{12,16},{16,20},{20,24},{24,28},{28,32},{32,36}... | collective-permute-start | bytes 6152 | tf_op jit(solution)/shard_map/ppermute | solution.py:17
  11.2 16.5 %collective-permute-start.2 = (s32[512]{0:T(512)}, s32[512]{0:T(512)S(1)}, u32[]{:S(2)}, u32[]{:S(2)}) collective-permute-start(s32[512]{0:T(512)} %param.20), channel_id=1, source_target_pairs={{0,8},{4,12},{8,16},{12,20},{16,24},{20,28},{24,32},{28,36},{32,40... | collective-permute-start | bytes 6152 | tf_op jit(solution)/shard_map/ppermute | solution.py:17
  23.7 4.0 copy-start.4
  30.2 34.0 %copy-start.5 = (f32[256]{0:T(256)S(1)}, f32[256]{0:T(256)}, u32[]{:S(2)}) copy-start(f32[256]{0:T(256)} %param.16) | copy-start | bytes 3076
  60.7 11.6 %copy-start.7 = (bf16[512,3840]{0,1:T(8,128)(2,1)S(1)}, bf16[512,3840]{0,1:T(8,128)(2,1)}, u32[]{:S(2)}) copy-start(bf16[512,3840]{0,1:T(8,128)(2,1)} %all-gather.4.cloned.1.call-done) | copy-start | bytes 11796484
  60.7 11.6 %copy-start.9 = (bf16[3840,256]{1,0:T(8,128)(2,1)S(1)}, bf16[3840,256]{1,0:T(8,128)(2,1)}, u32[]{:S(2)}) copy-start(bf16[3840,256]{1,0:T(8,128)(2,1)} %param.14) | copy-start | bytes 5898244
  66.2 169.1 %collective-permute-start.5 = (bf16[512,1,256]{0,2,1:T(8,128)(2,1)}, bf16[512,1,256]{0,2,1:T(8,128)(2,1)}, u32[]{:S(2)}, u32[]{:S(2)}) collective-permute-start(bf16[512,1,256]{0,2,1:T(8,128)(2,1)} %pad_maximum_fusion), channel_id=1, source_target_pairs={{0,4},{4,8},{8,12},{12,16},{16,20},{20,24},{24,28},{28,32},{32,36}... | collective-permute-start | bytes 786440 | tf_op jit(solution)/shard_map/ppermute | solution.py:17
  68.5 166.8 %collective-permute-start.4 = (bf16[512,1,256]{0,2,1:T(8,128)(2,1)}, bf16[512,1,256]{0,2,1:T(8,128)(2,1)}, u32[]{:S(2)}, u32[]{:S(2)}) collective-permute-start(bf16[512,1,256]{0,2,1:T(8,128)(2,1)} %pad_maximum_fusion), channel_id=1, source_target_pairs={{0,8},{4,12},{8,16},{12,20},{16,24},{20,28},{24,32},{28,36},{32,40... | collective-permute-start | bytes 786440 | tf_op jit(solution)/shard_map/ppermute | solution.py:17
  74.2 164.2 %collective-permute-start.1 = (bf16[512,1,256]{2,0,1:T(8,128)(2,1)}, bf16[512,1,256]{2,0,1:T(8,128)(2,1)}, u32[]{:S(2)}, u32[]{:S(2)}) collective-permute-start(bf16[512,1,256]{2,0,1:T(8,128)(2,1)} %fusion.34), channel_id=1, source_target_pairs={{0,4},{4,8},{8,12},{12,16},{16,20},{20,24},{24,28},{28,32},{32,36}... | collective-permute-start | bytes 786440 | tf_op jit(solution)/shard_map/ppermute | solution.py:17
  78.2 160.2 %collective-permute-start = (bf16[512,1,256]{2,0,1:T(8,128)(2,1)}, bf16[512,1,256]{2,0,1:T(8,128)(2,1)}, u32[]{:S(2)}, u32[]{:S(2)}) collective-permute-start(bf16[512,1,256]{2,0,1:T(8,128)(2,1)} %fusion.34), channel_id=1, source_target_pairs={{0,8},{4,12},{8,16},{12,20},{16,24},{20,28},{24,32},{28,36},{32,40... | collective-permute-start | bytes 786440 | tf_op jit(solution)/shard_map/ppermute | solution.py:17
  226.7 3.8 copy-start.6
  226.7 4.6 %copy-start.8 = (bf16[512,3840]{0,1:T(8,128)(2,1)S(1)}, bf16[512,3840]{0,1:T(8,128)(2,1)}, u32[]{:S(2)}) copy-start(bf16[512,3840]{0,1:T(8,128)(2,1)} %all-gather.4.cloned.1.call-done) | copy-start | bytes 11796484
  233.5 1.4 copy-start.3
  233.8 1.5 copy-start.2
  235.3 3.1 copy-start.10
  238.4 4.5 %copy-start.11 = (f32[1536,512,2]{1,0,2:T(8,128)}, f32[1536,512,2]{1,0,2:T(8,128)S(1)}, u32[]{:S(2)}) copy-start(f32[1536,512,2]{1,0,2:T(8,128)S(1)} %get-tuple-element.21) | copy-start | bytes 18874372
  253.0 149.6 %copy-start.1 = (bf16[3840,256]{1,0:T(8,128)(2,1)S(1)}, bf16[3840,256]{1,0:T(8,128)(2,1)}, u32[]{:S(2)}) copy-start(bf16[3840,256]{1,0:T(8,128)(2,1)} %param.13) | copy-start | bytes 5898244
Sparse Core Ops, SparseCore 0:
  9.8 50.8 all-gather.3
  63.4 84.3 all-gather.5
  150.6 76.0 all-gather.7
  253.1 149.4 reduce-scatter.1
where the time goes:
time: 410 us; the launch traced here: 409 us
  waiting for transfers between devices  295 us (72%)
  matrix products  44.1 us (11%)
  blocking collectives  20.2 us (5%)
  starting transfers between devices  18.7 us (5%)
  between operations  14.1 us (3%)
  other arithmetic  10.1 us (2%)
  local copies, waits for them, and re-layouts  6.79 us (2%)
    reduce_scatter x1, waiting for transfers between devices, local(): lax.psum_scatter(jnp.einsum('acr,ace->are', slot_low_rows, slot_grad_rows...  143 us
    all_gather x1, waiting for transfers between devices, local(): lax.all_gather(adapter_down, 'seq', axis=0, tiled=True)  66.8 us
    all_gather x1, waiting for transfers between devices, local(): lax.all_gather(adapter_up, 'seq', axis=0, tiled=True)  52.3 us
    all_gather x1, waiting for transfers between devices, local(): shard_cols = lax.all_gather(tokens, 'tensor', axis=1, tiled=True)  30.4 us
    psum x1, blocking collectives, local(): slot_low = lax.psum(partial_low, 'tensor').astype(jnp.bfloat16)  20.2 us
    ppermute x6, starting transfers between devices, passed_along(): lax.ppermute(value, axis, [(source, source + steps) for source in range(f...  18.6 us
  transfers between devices with their start and end apart: 10, of which 4 were waited for; matrix products, arithmetic and copies ran while one was open for 11% of the time, Pallas kernels for 0%

commit v1 on v0

--- a/solution.py
+++ b/solution.py
@@ -9,6 +9,12 @@
 WINDOW = 1024
 ADAPTERS = 64
 CAP = 16
+
+
+def _note_shards(raw, in_dim):
+    extra = list(raw.shape[1:])
+    extra[in_dim] *= raw.shape[0]
+    return jnp.moveaxis(raw, 0, in_dim).reshape(extra)
 
 
 def passed_along(value, axis, steps):
@@ -80,7 +86,25 @@
     kv_heads = kv_width // HD
     head_group = local_heads // kv_heads
     positions = lax.axis_index("seq") * tok_count + jnp.arange(tok_count, dtype=jnp.int32)
-    shard_cols = lax.all_gather(tokens, "tensor", axis=1, tiled=True)
+    width = lax.psum(1, "tensor")
+    store = [(nth, (nth + 1) % width) for nth in range(width)]
+    d_next, after = ([], [])
+    m = 0
+    pieces_in = [(ix, b) for b, ix in store]
+    while m < width - 1:
+        if m % 2 == 0:
+            raw_out = lax.ppermute(d_next[-1] if d_next else tokens, "tensor", store)
+            d_next.append(raw_out)
+        else:
+            n_now = lax.ppermute(after[-1] if after else tokens, "tensor", pieces_in)
+            after.append(n_now)
+        m += 1
+    m_next = jnp.stack([*d_next[::-1], tokens, *after], axis=0)
+    plain = lax.axis_index("tensor")
+    p_next = len(d_next)
+    h_now = plain - p_next
+    m_next = m_next[(jnp.arange(width) - h_now) % width]
+    shard_cols = _note_shards(m_next, 1)
     query_lin = jnp.dot(shard_cols, w_query, preferred_element_type=jnp.float32)
     key_lin = jnp.dot(shard_cols, w_key, preferred_element_type=jnp.float32)
     value_lin = jnp.dot(shard_cols, w_value, preferred_element_type=jnp.float32)

time: 410 us -> 362 us (0.88)
  waiting for transfers between devices: 295 us -> 234 us
  local copies, waits for them, and re-layouts: 6.79 us -> 11.6 us
  starting transfers between devices: 18.7 us -> 23.3 us
    all_gather x1, waiting for transfers between devices: 66.8 us -> 4.1 us  [local(): lax.all_gather(adapter_down, 'seq', axis=0, tiled=True)]
    ppermute x0 -> x3, waiting for transfers between devices: none -> 33.8 us  [the longest x2 33.8 us: local(): raw_out = lax.ppermute(d_next[-1] if d_next else tokens, 'tensor', store)]
    all_gather x1 -> x0, waiting for transfers between devices: 30.4 us -> none  [local(): shard_cols = lax.all_gather(tokens, 'tensor', axis=1, tiled=True)]
    gather x0 -> x1, local copies, waits for them, and re-layouts: none -> 4.9 us  [local(): m_next = m_next[(jnp.arange(width) - h_now) % width]]
  transfers between devices with their start and end apart: 10 -> 12, of which waited for: 4 -> 5; matrix products, arithmetic and copies ran while one was open for 11% -> 15% of each run, Pallas kernels for 0% -> 0%
where the time goes in v1:
time: 362 us; the launch traced here: 361 us
  waiting for transfers between devices  234 us (65%)
  matrix products  44.1 us (12%)
  starting transfers between devices  23.3 us (6%)
  blocking collectives  20.7 us (6%)
  between operations  14.1 us (4%)
  other arithmetic  13.7 us (4%)
  local copies, waits for them, and re-layouts  11.6 us (3%)
    reduce_scatter x1, waiting for transfers between devices, local(): lax.psum_scatter(jnp.einsum('acr,ace->are', slot_low_rows, slot_grad_rows...  143 us
    all_gather x1, waiting for transfers between devices, local(): lax.all_gather(adapter_up, 'seq', axis=0, tiled=True)  51 us
    ppermute x2, waiting for transfers between devices, local(): raw_out = lax.ppermute(d_next[-1] if d_next else tokens, 'tensor', store)  33.8 us
    psum x1, blocking collectives, local(): slot_low = lax.psum(partial_low, 'tensor').astype(jnp.bfloat16)  20.7 us
    ppermute x6, starting transfers between devices, passed_along(): lax.ppermute(value, axis, [(source, source + steps) for source in range(f...  20 us
  transfers between devices with their start and end apart: 12, of which 5 were waited for; matrix products, arithmetic and copies ran while one was open for 15% of the time, Pallas kernels for 0%

profile of v1, /device:TPU:2, one launch (start us, length us, event | category | flops | bytes accessed | tf_op | source)
XLA Modules:
  0.0 361.2 jit_solution(6627960136760291712)
XLA Ops:
  8.7 1.7 collective-permute-start.6
  10.5 4.0 %collective-permute-start.5 = (s32[512]{0:T(512)}, s32[512]{0:T(512)S(1)}, u32[]{:S(2)}, u32[]{:S(2)}) collective-permute-start(s32[512]{0:T(512)} %param.20), channel_id=1, source_target_pairs={{0,8},{4,12},{8,16},{12,20},{16,24},{20,28},{24,32},{28,36},{32,40... | collective-permute-start | bytes 6152 | tf_op jit(solution)/shard_map/ppermute | solution.py:23
  15.1 1.5 collective-permute-start
  17.3 1.2 reduce-window.6
  20.3 3.8 %fusion.24 = bf16[1024,960]{0,1:T(8,128)(2,1)} fusion(bf16[512,960]{0,1:T(8,128)(2,1)} %param.11, s32[512]{0:T(512)S(1)} %multiply_add_fusion.3), kind=kOutput, calls=%fused_computation.29 | convolution fusion | flops 1008140288 | bytes 2951168 | tf_op jit(solution)/shard_map/dot_general | solution.py:119
  24.1 16.0 %collective-permute-done = bf16[512,960]{0,1:T(8,128)(2,1)} collective-permute-done((bf16[512,960]{0,1:T(8,128)(2,1)}, bf16[512,960]{0,1:T(8,128)(2,1)}, u32[]{:S(2)}, u32[]{:S(2)}) %collective-permute-start) | collective-permute-done | bytes 983072 | tf_op jit(solution)/shard_map/ppermute | solution.py:96
  40.0 1.0 collective-permute-start.1
  42.0 3.9 %copy.40 = bf16[1024,960]{1,0:T(8,128)(2,1)} copy(bf16[1024,960]{0,1:T(8,128)(2,1)} %fusion.24) | data formatting | bytes 3932160 | tf_op jit(solution)/shard_map/convert_element_type | solution.py:119
  46.0 2.5 fusion.16
  48.5 17.8 %collective-permute-done.1 = bf16[512,960]{0,1:T(8,128)(2,1)} collective-permute-done((bf16[512,960]{0,1:T(8,128)(2,1)}, bf16[512,960]{0,1:T(8,128)(2,1)}, u32[]{:S(2)}, u32[]{:S(2)}) %collective-permute-start.1) | collective-permute-done | bytes 983072 | tf_op jit(solution)/shard_map/ppermute | solution.py:96
  66.3 3.5 pad_maximum_fusion
  69.9 4.9 %gather_fusion = bf16[4,512,960]{1,2,0:T(8,128)(2,1)} fusion(bf16[4,512,960]{1,2,0:T(8,128)(2,1)} %pad_maximum_fusion, s32[1024]{0:T(1024)S(1)} %pad_clamp_fusion), kind=kCustom, calls=%fused_computation | custom fusion | bytes 7864336 | tf_op jit(solution)/shard_map/gather | solution.py:106
  74.8 3.5 multiply_reduce_fusion.2
  78.5 1.2 fusion.55
  80.4 2.6 collective-permute-start.8
  83.0 3.5 collective-permute-start.7
  86.5 1.9 fusion.34
  88.4 2.6 collective-permute-start.4
  91.0 5.6 %collective-permute-start.3 = (bf16[512,1,256]{2,0,1:T(8,128)(2,1)}, bf16[512,1,256]{2,0,1:T(8,128)(2,1)}, u32[]{:S(2)}, u32[]{:S(2)}) collective-permute-start(bf16[512,1,256]{2,0,1:T(8,128)(2,1)} %fusion.34), channel_id=1, source_target_pairs={{0,8},{4,12},{8,16},{12,20},{16,24},{20,28},{24,32},{28,36},{32,40... | collective-permute-start | bytes 786440 | tf_op jit(solution)/shard_map/ppermute | solution.py:23
  96.6 4.1 %all-gather.3.cloned.1.call-done = bf16[64,64,960]{2,1,0:T(8,128)(2,1)} async-done(((bf16[1,64,960]{2,1,0:T(8,128)(2,1)}), bf16[64,64,960]{2,1,0:T(8,128)(2,1)}) %all-gather.3.cloned.1.call-update) | async-done | bytes 7864336 | tf_op jit(solution)/shard_map/all_gather | solution.py:121
  100.7 6.3 %fusion.75 = f32[64,16,64]{2,1,0:T(8,128)S(1)} fusion(bf16[64,16,960]{2,1,0:T(8,128)(2,1)} %bitcast.137, bf16[64,64,960]{2,1,0:T(8,128)(2,1)} %all-gather.3.cloned.1.call-done), kind=kOutput, calls=%fused_computation.115 | convolution fusion | flops 125829120 | bytes 10092544 | tf_op jit(solution)/shard_map/acd,ard->acr/dot_general | solution.py:125
  107.0 20.7 %all-reduce.3 = bf16[64,16,64]{2,1,0:T(8,128)(2,1)S(1)} all-reduce(f32[64,16,64]{2,1,0:T(8,128)S(1)} %fusion.75), channel_id=1, replica_groups=mesh['seq'=64,'tensor'=4] {'tensor'}, use_global_device_ids=true, to_apply=%region_4.5 | all-reduce | flops 65536 | bytes 393216 | tf_op jit(solution)/shard_map/psum | solution.py:128
  127.7 51.0 %all-gather.5.cloned.1.call-done = bf16[64,64,512]{2,1,0:T(8,128)(2,1)} async-done(((bf16[1,64,512]{2,1,0:T(8,128)(2,1)}), bf16[64,64,512]{2,1,0:T(8,128)(2,1)}) %all-gather.5.cloned.1.call-update) | async-done | bytes 4194320 | tf_op jit(solution)/shard_map/all_gather | solution.py:122
  178.8 3.0 convolution_convert_fusion
  183.3 2.3 multiply_reduce_fusion.1
  187.5 3.1 fusion.5
  190.6 4.4 %fusion = (f32[2,512]{1,0:T(2,128)S(1)}, f32[1536,512,2]{1,0,2:T(8,128)S(1)}) fusion(f32[2,512]{1,0:T(2,128)S(1)} %get-tuple-element.20, f32[1536,512,2]{1,0,2:T(8,128)S(1)} %get-tuple-element.21, pred[512,1536]{0,1:T(8,128)(4,1)S(1)} %copy-done.5, bf16[64,2,8,256]{3,2,1,0:T(8,128)(2,1)S(1)} %bitcast.152, bf16[512,1,256]{2,0,1:T(8,128)(2,1)} %fusion.34, ...), kind=kOutput, calls=%fused_computation.4 | convolution fusion | flops 815528960 | bytes 14688256 | tf_op jit(solution)/shard_map/tngd,knd->ngtk/dot_general | solution.py:61
  195.0 3.8 %fusion.26 = f32[512,2,256]{2,0,1:T(8,128)S(1)} fusion(f32[1536,512,2]{1,0,2:T(8,128)S(1)} %get-tuple-element.23, f32[2,512]{1,0:T(2,128)S(1)} %get-tuple-element.22, f32[2,512]{1,0:T(2,128)S(1)} %get-tuple-element.20, f32[1536,512,2]{1,0,2:T(8,128)S(1)} %get-tuple-element.21, pred[512,1536]{0,1:T(8,128)(4,1)S(1)} %copy-done.5, ...), kind=kOutput, calls=%fused_computation.33 | convolution fusion | flops 819462144 | bytes 15212544 | tf_op jit(solution)/shard_map/ngtk,knd->tngd/dot_general | solution.py:64
  200.6 4.5 %fusion.76 = f32[64,64,512]{2,1,0:T(8,128)} fusion(bf16[64,16,64]{2,1,0:T(8,128)(2,1)S(1)} %bitcast.142, bf16[64,16,512]{2,1,0:T(8,128)(2,1)S(1)} %bitcast.141), kind=kOutput, calls=%fused_computation.116 | convolution fusion | flops 67108864 | bytes 9568256 | tf_op jit(solution)/shard_map/acr,ace->are/dot_general | solution.py:191
  205.1 5.2 %fusion.31 = bf16[256,2,512]{2,0,1:T(8,128)(2,1)S(1)} fusion(f32[2,512]{1,0:T(2,128)S(1)} %get-tuple-element.20, f32[1536,512,2]{1,0,2:T(8,128)} %copy-done.12, pred[512,1536]{0,1:T(8,128)(4,1)S(1)} %copy-done.5, bf16[512,1,256]{2,0,1:T(8,128)(2,1)} %fusion.34, bf16[512,1,256]{2,0,1:T(8,128)(2,1)} %collective-permute-done.4, ...), kind=kOutput, calls=%fused_computation.37 | convolution fusion | flops 814219264 | bytes 8392704 | tf_op jit(solution)/shard_map/ngtk,knd->tngd/dot_general | solution.py:60
  210.3 1.0 copy.52
  211.3 143.4 %reduce-scatter.2.cloned.1.call-done = f32[1,64,512]{2,1,0:T(8,128)} async-done(((f32[64,64,512]{2,1,0:T(8,128)}), f32[1,64,512]{2,1,0:T(8,128)}) %reduce-scatter.2.cloned.1.call-update) | async-done | bytes 131088 | tf_op jit(solution)/shard_map/reduce_scatter | solution.py:190
  (72 shorter events, 11.6 us)
Async XLA Ops:
  7.2 67.6 %copy-start = (bf16[3840,256]{1,0:T(8,128)(2,1)S(1)}, bf16[3840,256]{1,0:T(8,128)(2,1)}, u32[]{:S(2)}) copy-start(bf16[3840,256]{1,0:T(8,128)(2,1)} %param.13) | copy-start | bytes 5898244
  7.2 93.5 %all-gather.3.cloned.1.call-start = ((), (), s32[]{:S(2)}) async-start(), calls=%async_computation.1 | async-start | bytes 8519680 | tf_op jit(solution)/shard_map/all_gather | solution.py:121
  7.9 170.9 %all-gather.5.cloned.1.call-start = ((), (), s32[]{:S(2)}) async-start(), calls=%async_computation.2 | async-start | bytes 4259840 | tf_op jit(solution)/shard_map/all_gather | solution.py:122
  8.7 346.0 %reduce-scatter.2.cloned.1.call-start = ((), (), s32[]{:S(2)}) async-start(), calls=%async_computation.3 | async-start | bytes 8519680 | tf_op jit(solution)/shard_map/reduce_scatter | solution.py:190
  8.7 37.3 %collective-permute-start.6 = (s32[512]{0:T(512)}, s32[512]{0:T(512)S(1)}, u32[]{:S(2)}, u32[]{:S(2)}) collective-permute-start(s32[512]{0:T(512)} %param.20), channel_id=1, source_target_pairs={{0,4},{4,8},{8,12},{12,16},{16,20},{20,24},{24,28},{28,32},{32,36}... | collective-permute-start | bytes 6152 | tf_op jit(solution)/shard_map/ppermute | solution.py:23
  10.5 35.5 %collective-permute-start.5 = (s32[512]{0:T(512)}, s32[512]{0:T(512)S(1)}, u32[]{:S(2)}, u32[]{:S(2)}) collective-permute-start(s32[512]{0:T(512)} %param.20), channel_id=1, source_target_pairs={{0,8},{4,12},{8,16},{12,20},{16,24},{20,28},{24,32},{28,36},{32,40... | collective-permute-start | bytes 6152 | tf_op jit(solution)/shard_map/ppermute | solution.py:23
  14.5 34.0 %collective-permute-start.2 = (bf16[512,960]{0,1:T(8,128)(2,1)}, bf16[512,960]{0,1:T(8,128)(2,1)}, u32[]{:S(2)}, u32[]{:S(2)}) collective-permute-start(bf16[512,960]{0,1:T(8,128)(2,1)} %param.11), channel_id=1, source_target_pairs={{1,0},{2,1},{3,2},{0,3},{5,4},{6,5},{7,6},{4,7},{9,8},{10,9},{11,1... | collective-permute-start | bytes 2949128 | tf_op jit(solution)/shard_map/ppermute | solution.py:99
  15.1 24.9 %collective-permute-start = (bf16[512,960]{0,1:T(8,128)(2,1)}, bf16[512,960]{0,1:T(8,128)(2,1)}, u32[]{:S(2)}, u32[]{:S(2)}) collective-permute-start(bf16[512,960]{0,1:T(8,128)(2,1)} %param.11), channel_id=1, source_target_pairs={{0,1},{1,2},{2,3},{3,0},{4,5},{5,6},{6,7},{7,4},{8,9},{9,10},{10,1... | collective-permute-start | bytes 2949128 | tf_op jit(solution)/shard_map/ppermute | solution.py:96
  24.1 21.9 %copy-start.7 = (s32[512]{0:T(512)S(1)}, s32[512]{0:T(512)}, u32[]{:S(2)}) copy-start(s32[512]{0:T(512)} %param.20) | copy-start | bytes 6148
  24.1 42.3 %copy-start.4 = (bf16[512,960]{0,1:T(8,128)(2,1)S(1)}, bf16[512,960]{0,1:T(8,128)(2,1)}, u32[]{:S(2)}) copy-start(bf16[512,960]{0,1:T(8,128)(2,1)} %param.11) | copy-start | bytes 2949124
  40.0 26.3 %collective-permute-start.1 = (bf16[512,960]{0,1:T(8,128)(2,1)}, bf16[512,960]{0,1:T(8,128)(2,1)}, u32[]{:S(2)}, u32[]{:S(2)}) collective-permute-start(bf16[512,960]{0,1:T(8,128)(2,1)} %collective-permute-done), channel_id=1, source_target_pairs={{0,1},{1,2},{2,3},{3,0},{4,5},{5,6},{6,7},{7,4},{8,9},{9,10},{10,1... | collective-permute-start | bytes 2949128 | tf_op jit(solution)/shard_map/ppermute | solution.py:96
  74.8 3.6 copy-start.8
  74.8 11.7 %copy-start.2 = (bf16[4,512,960]{1,2,0:T(8,128)(2,1)S(1)}, bf16[4,512,960]{1,2,0:T(8,128)(2,1)}, u32[]{:S(2)}) copy-start(bf16[4,512,960]{1,2,0:T(8,128)(2,1)} %gather_fusion) | copy-start | bytes 11796484
  74.8 11.7 %copy-start.10 = (bf16[3840,256]{1,0:T(8,128)(2,1)S(1)}, bf16[3840,256]{1,0:T(8,128)(2,1)}, u32[]{:S(2)}) copy-start(bf16[3840,256]{1,0:T(8,128)(2,1)} %param.14) | copy-start | bytes 5898244
  80.4 107.0 %collective-permute-start.8 = (bf16[512,1,256]{0,2,1:T(8,128)(2,1)}, bf16[512,1,256]{0,2,1:T(8,128)(2,1)}, u32[]{:S(2)}, u32[]{:S(2)}) collective-permute-start(bf16[512,1,256]{0,2,1:T(8,128)(2,1)} %pad_maximum_fusion.1), channel_id=1, source_target_pairs={{0,4},{4,8},{8,12},{12,16},{16,20},{20,24},{24,28},{28,32},{32,36}... | collective-permute-start | bytes 786440 | tf_op jit(solution)/shard_map/ppermute | solution.py:23
  83.0 104.4 %collective-permute-start.7 = (bf16[512,1,256]{0,2,1:T(8,128)(2,1)}, bf16[512,1,256]{0,2,1:T(8,128)(2,1)}, u32[]{:S(2)}, u32[]{:S(2)}) collective-permute-start(bf16[512,1,256]{0,2,1:T(8,128)(2,1)} %pad_maximum_fusion.1), channel_id=1, source_target_pairs={{0,8},{4,12},{8,16},{12,20},{16,24},{20,28},{24,32},{28,36},{32,40... | collective-permute-start | bytes 786440 | tf_op jit(solution)/shard_map/ppermute | solution.py:23
  88.4 102.1 %collective-permute-start.4 = (bf16[512,1,256]{2,0,1:T(8,128)(2,1)}, bf16[512,1,256]{2,0,1:T(8,128)(2,1)}, u32[]{:S(2)}, u32[]{:S(2)}) collective-permute-start(bf16[512,1,256]{2,0,1:T(8,128)(2,1)} %fusion.34), channel_id=1, source_target_pairs={{0,4},{4,8},{8,12},{12,16},{16,20},{20,24},{24,28},{28,32},{32,36}... | collective-permute-start | bytes 786440 | tf_op jit(solution)/shard_map/ppermute | solution.py:23
  91.0 99.6 %collective-permute-start.3 = (bf16[512,1,256]{2,0,1:T(8,128)(2,1)}, bf16[512,1,256]{2,0,1:T(8,128)(2,1)}, u32[]{:S(2)}, u32[]{:S(2)}) collective-permute-start(bf16[512,1,256]{2,0,1:T(8,128)(2,1)} %fusion.34), channel_id=1, source_target_pairs={{0,8},{4,12},{8,16},{12,20},{16,24},{20,28},{24,32},{28,36},{32,40... | collective-permute-start | bytes 786440 | tf_op jit(solution)/shard_map/ppermute | solution.py:23
  178.8 3.8 %copy-start.3 = (bf16[4,512,960]{1,2,0:T(8,128)(2,1)S(1)}, bf16[4,512,960]{1,2,0:T(8,128)(2,1)}, u32[]{:S(2)}) copy-start(bf16[4,512,960]{1,2,0:T(8,128)(2,1)} %gather_fusion) | copy-start | bytes 11796484
  178.8 4.6 %copy-start.9 = (bf16[3840,512]{1,0:T(8,128)(2,1)S(1)}, bf16[3840,512]{1,0:T(8,128)(2,1)}, u32[]{:S(2)}) copy-start(bf16[3840,512]{1,0:T(8,128)(2,1)} %param.12) | copy-start | bytes 11796484
  185.6 1.4 copy-start.6
  186.0 1.5 copy-start.5
  187.4 3.1 copy-start.11
  190.5 4.5 %copy-start.12 = (f32[1536,512,2]{1,0,2:T(8,128)}, f32[1536,512,2]{1,0,2:T(8,128)S(1)}, u32[]{:S(2)}) copy-start(f32[1536,512,2]{1,0,2:T(8,128)S(1)} %get-tuple-element.21) | copy-start | bytes 18874372
  205.1 149.6 %copy-start.1 = (bf16[3840,256]{1,0:T(8,128)(2,1)S(1)}, bf16[3840,256]{1,0:T(8,128)(2,1)}, u32[]{:S(2)}) copy-start(bf16[3840,256]{1,0:T(8,128)(2,1)} %param.13) | copy-start | bytes 5898244
Sparse Core Ops, SparseCore 0:
  10.8 89.8 all-gather.2
  103.5 75.2 all-gather.4
  205.2 149.4 reduce-scatter.1
